TPU v7x, 32 devices: a whole 2x2x4 slice. The times are simulated.
32 devices in a mesh: slab: 2 (over x), blk: 16 (over z, y, core).
Axes of the slice: x: 2, y: 2, z: 4, core: 2. Of those that a mesh axis runs over, the one named last changes fastest.
Arguments:
- transmit: bfloat16 [2, 1024, 2048], P('slab', 'blk'), may hold values from -0.125 to 0.125
- reflect: bfloat16 [2, 2, 1024, 2048], P('slab', None, 'blk'), may hold values from -0.07910156 to 0.07910156
- source_amp: bfloat16 [512, 2048], P('blk'), may hold values from -6 to 6
- source_cell: int32 [512], P('blk'), may hold values from 0 to 1023
- source_slab: int32 [512], P('blk'), may hold values from 0 to 1
Outputs:
- sweep_out: float32 [2, 512, 2048], P('slab', 'blk')
All inputs are finite; a program needn't handle non-finite values.
Results may differ from a plain program's by a relative error of at most 0.018.
Values may be sent and summed in bfloat16 or wider, within the bound.
A program may use at most 64 MiB of HBM per device.

v0:
```python
import jax
import jax.numpy as jnp
from jax import lax
from jax.sharding import PartitionSpec as P


def shifted(block, axis, distance):
    devices = range(lax.axis_size(axis))
    route = [(i - distance, i) for i in devices if i - distance in devices]
    return lax.ppermute(block, axis, route)


def transposed(matrix):
    half_width = matrix.shape[0]
    return jnp.concatenate([matrix[:, :half_width].T, matrix[:, half_width:].T], 1)


def complex_rows(left_rows, right_matrix):
    inner_width = right_matrix.shape[0]
    outer_width = right_matrix.shape[1] // 2
    row_count = left_rows.shape[0]
    stacked = jnp.concatenate([left_rows[:, :inner_width], left_rows[:, inner_width:]], 0)
    product = jnp.dot(stacked, right_matrix, preferred_element_type=jnp.float32)
    real_out = product[:row_count, :outer_width] - product[row_count:, outer_width:]
    imag_out = product[:row_count, outer_width:] + product[row_count:, :outer_width]
    return jnp.concatenate([real_out, imag_out], 1)


def body(transmit, reflect, source_amp, source_cell, source_slab):
    trans_local = transmit[0]
    refl_local = reflect[0]
    half_width = source_amp.shape[1] // 2
    refl_second = lax.all_gather(refl_local[1], "blk", axis=0, tiled=True)
    coupling = complex_rows(refl_local[0], refl_second).astype(jnp.bfloat16)
    start_rows = trans_local.astype(jnp.float32)
    piece_rows = lax.all_gather(trans_local, "blk", axis=0, tiled=True)
    piece_count = piece_rows.shape[0]
    real_cols = lax.slice_in_dim(coupling, 0, piece_count, axis=1)
    imag_cols = lax.dynamic_slice_in_dim(coupling, half_width, piece_count, 1)
    left_rows = jnp.concatenate([real_cols, imag_cols], 1)
    joined = (start_rows + complex_rows(left_rows, piece_rows)).astype(jnp.bfloat16)
    slab_matrix = lax.all_gather(joined, "blk", axis=0, tiled=True)
    back_matrix = transposed(slab_matrix)
    cell_index = lax.iota(jnp.int32, half_width)
    offset = (cell_index[None, :] - source_cell[:, None]) % half_width
    inside = offset < half_width // 4
    here = source_slab == lax.axis_index("slab")
    keep = inside & here[:, None]
    keep = jnp.concatenate([keep, keep], 1)
    forcing = jnp.where(keep, source_amp, jnp.zeros_like(source_amp))
    chain_length = lax.axis_size("slab")
    carried = forcing
    for sweep_step in range(chain_length - 1):
        arrived = shifted(carried, "slab", 1)
        carried = (forcing.astype(jnp.float32) + complex_rows(arrived, slab_matrix)).astype(
            jnp.bfloat16
        )
    current = carried.astype(jnp.float32)
    for sweep_step in range(chain_length - 1):
        message = complex_rows(current.astype(jnp.bfloat16), back_matrix).astype(jnp.bfloat16)
        arrived = shifted(message, "slab", -1)
        current = carried.astype(jnp.float32) + arrived.astype(jnp.float32)
    return current[None]


def solution(mesh):
    return jax.shard_map(
        body,
        mesh=mesh,
        in_specs=(
            P("slab", "blk", None),
            P("slab", None, "blk", None),
            P("blk", None),
            P("blk"),
            P("blk"),
        ),
        out_specs=P("slab", "blk", None),
        check_vma=False,
    )
```

profile of v0, /device:TPU:0, one launch (start us, length us, event | category | flops | bytes accessed | tf_op | source)
XLA Modules:
  0.0 186.9 jit_solution(4141823036874665269)
XLA Ops:
  6.5 1.8 slice_bitcast_fusion.2
  8.3 0.0 all-gather.8.cloned.1.call-update
  8.3 0.0 all-gather.10.cloned.1.call-start
  8.4 0.7 all-gather.10.cloned.1.call-update
  9.1 0.0 all-gather.6.cloned.1.call-start
  9.2 53.5 %all-gather.8.cloned.1.call-done = bf16[1,1,1024,2048]{3,2,1,0:T(8,128)(2,1)} async-done(((bf16[1,1,64,2048]{3,2,1,0:T(8,128)(2,1)}), bf16[1,1,1024,2048]{3,2,1,0:T(8,128)(2,1)}) %all-gather.8.cloned.1.call-update) | async-done | bytes 4194320 | tf_op jit(solution)/shard_map/all_gather | solution.py:33
  62.6 2.9 %fusion.6 = f32[128,2048]{1,0:T(8,128)S(1)} fusion(bf16[1,1,1024,2048]{3,2,1,0:T(8,128)(2,1)} %all-gather.8.cloned.1.call-done, bf16[64,1024]{1,0:T(8,128)(2,1)S(1)} %get-tuple-element.18, bf16[64,1024]{1,0:T(8,128)(2,1)S(1)} %get-tuple-element.17), kind=kOutput, calls=%fused_computation.6 | convolution fusion | flops 537395200 | bytes 5505024 | tf_op jit(solution)/shard_map/dot_general | solution.py:23
  65.5 0.1 fusion.10
  65.6 48.1 %all-gather.10.cloned.1.call-done = bf16[1,1024,2048]{2,1,0:T(8,128)(2,1)} async-done(((bf16[1,64,2048]{2,1,0:T(8,128)(2,1)}), bf16[1,1024,2048]{2,1,0:T(8,128)(2,1)}) %all-gather.10.cloned.1.call-update) | async-done | bytes 4194320 | tf_op jit(solution)/shard_map/all_gather | solution.py:36
  113.7 2.9 %fusion.4 = f32[128,2048]{1,0:T(8,128)S(1)} fusion(bf16[1,1024,2048]{2,1,0:T(8,128)(2,1)} %all-gather.10.cloned.1.call-done, bf16[64,1024]{1,0:T(8,128)(2,1)S(1)} %get-tuple-element.10, bf16[64,1024]{1,0:T(8,128)(2,1)S(1)} %get-tuple-element.9), kind=kOutput, calls=%fused_computation.4 | convolution fusion | flops 537395200 | bytes 5505024 | tf_op jit(solution)/shard_map/dot_general | solution.py:23
  116.7 0.1 slice_subtract_fusion
  116.8 0.8 fusion.8
  117.5 0.0 all-gather.6.cloned.1.call-update
  117.6 0.1 fusion.32
  117.8 3.4 %collective-permute-start = (bf16[32,2048]{1,0:T(8,128)(2,1)S(1)}, bf16[32,2048]{1,0:T(8,128)(2,1)S(1)}, u32[]{:S(2)}, u32[]{:S(2)}) collective-permute-start(bf16[32,2048]{1,0:T(8,128)(2,1)S(1)} %add_select_fusion), channel_id=1, source_target_pairs={{0,16},{1,17},{2,18},{3,19},{4,20},{5,21},{6,22},{7,23},{8,24},{9,... | collective-permute-start | bytes 393224 | tf_op jit(solution)/shard_map/ppermute | solution.py:10
  121.2 3.1 %collective-permute-done = bf16[32,2048]{1,0:T(8,128)(2,1)S(1)} collective-permute-done((bf16[32,2048]{1,0:T(8,128)(2,1)S(1)}, bf16[32,2048]{1,0:T(8,128)(2,1)S(1)}, u32[]{:S(2)}, u32[]{:S(2)}) %collective-permute-start) | collective-permute-done | bytes 131104 | tf_op jit(solution)/shard_map/ppermute | solution.py:10
  124.3 42.3 %all-gather.6.cloned.1.call-done = bf16[1024,2048]{1,0:T(8,128)(2,1)} async-done(((bf16[64,2048]{1,0:T(8,128)(2,1)}), bf16[1024,2048]{1,0:T(8,128)(2,1)}) %all-gather.6.cloned.1.call-update) | async-done | bytes 4194320 | tf_op jit(solution)/shard_map/all_gather | solution.py:42
  166.6 3.2 %fusion.22 = f32[64,2048]{1,0:T(8,128)S(1)} fusion(bf16[1024,2048]{1,0:T(8,128)(2,1)} %all-gather.6.cloned.1.call-done, bf16[32,1024]{1,0:T(8,128)(2,1)S(1)} %get-tuple-element.22, bf16[32,1024]{1,0:T(8,128)(2,1)S(1)} %get-tuple-element.21), kind=kOutput, calls=%fused_computation.40 | convolution fusion | flops 268697600 | bytes 4849664 | tf_op jit(solution)/shard_map/dot_general | solution.py:23
  169.9 0.2 copy-done
  170.1 0.5 slice_bitcast_fusion.1
  170.6 1.4 fusion
  172.1 1.3 collective-permute-start.1
  173.4 6.2 %collective-permute-done.1 = bf16[32,2048]{1,0:T(8,128)(2,1)S(1)} collective-permute-done((bf16[32,2048]{1,0:T(8,128)(2,1)S(1)}, bf16[32,2048]{1,0:T(8,128)(2,1)S(1)}, u32[]{:S(2)}, u32[]{:S(2)}) %collective-permute-start.1) | collective-permute-done | bytes 131104 | tf_op jit(solution)/shard_map/ppermute | solution.py:10
  179.6 0.7 add_bitcast_fusion
  (19 shorter events, 0.2 us)
Async XLA Ops:
  6.5 56.1 %all-gather.8.cloned.1.call-start = ((), (), s32[]{:S(2)}) async-start(), calls=%async_computation.1 | async-start | bytes 4456448 | tf_op jit(solution)/shard_map/all_gather | solution.py:33
  8.3 105.4 %all-gather.10.cloned.1.call-start = ((), (), s32[]{:S(2)}) async-start(), calls=%async_computation.2 | async-start | bytes 4456448 | tf_op jit(solution)/shard_map/all_gather | solution.py:36
  9.1 157.5 %all-gather.6.cloned.1.call-start = ((), (), s32[]{:S(2)}) async-start(), calls=%async_computation | async-start | bytes 4456448 | tf_op jit(solution)/shard_map/all_gather | solution.py:42
  65.5 51.2 %copy-start.1 = (bf16[1,64,2048]{2,1,0:T(8,128)(2,1)S(1)}, bf16[1,64,2048]{2,1,0:T(8,128)(2,1)}, u32[]{:S(2)}) copy-start(bf16[1,64,2048]{2,1,0:T(8,128)(2,1)} %param.5) | copy-start | bytes 786436
  113.7 3.8 %copy-start.4 = (s32[32]{0:T(128)S(1)}, s32[32]{0:T(128)}, u32[]{:S(2)}) copy-start(s32[32]{0:T(128)} %param.9) | copy-start | bytes 388
  113.7 3.9 %copy-start.3 = (s32[32]{0:T(128)S(1)}, s32[32]{0:T(128)}, u32[]{:S(2)}) copy-start(s32[32]{0:T(128)} %param.8) | copy-start | bytes 388
  113.7 4.0 %copy-start.2 = (bf16[32,2048]{1,0:T(8,128)(2,1)S(1)}, bf16[32,2048]{1,0:T(8,128)(2,1)}, u32[]{:S(2)}) copy-start(bf16[32,2048]{1,0:T(8,128)(2,1)} %param.7) | copy-start | bytes 393220
  117.8 6.5 %collective-permute-start = (bf16[32,2048]{1,0:T(8,128)(2,1)S(1)}, bf16[32,2048]{1,0:T(8,128)(2,1)S(1)}, u32[]{:S(2)}, u32[]{:S(2)}) collective-permute-start(bf16[32,2048]{1,0:T(8,128)(2,1)S(1)} %add_select_fusion), channel_id=1, source_target_pairs={{0,16},{1,17},{2,18},{3,19},{4,20},{5,21},{6,22},{7,23},{8,24},{9,... | collective-permute-start | bytes 393224 | tf_op jit(solution)/shard_map/ppermute | solution.py:10
  166.6 3.4 %copy-start = (bf16[1024,2048]{1,0:T(8,128)(2,1)S(1)}, bf16[1024,2048]{1,0:T(8,128)(2,1)}, u32[]{:S(2)}) copy-start(bf16[1024,2048]{1,0:T(8,128)(2,1)} %all-gather.6.cloned.1.call-done) | copy-start | bytes 12582916
  172.1 7.5 %collective-permute-start.1 = (bf16[32,2048]{1,0:T(8,128)(2,1)S(1)}, bf16[32,2048]{1,0:T(8,128)(2,1)S(1)}, u32[]{:S(2)}, u32[]{:S(2)}) collective-permute-start(bf16[32,2048]{1,0:T(8,128)(2,1)S(1)} %pad_maximum_fusion), channel_id=1, source_target_pairs={{16,0},{17,1},{18,2},{19,3},{20,4},{21,5},{22,6},{23,7},{24,8},{25... | collective-permute-start | bytes 393224 | tf_op jit(solution)/shard_map/ppermute | solution.py:10
Sparse Core Ops, SparseCore 0:
  9.5 53.0 all-gather.7
  64.8 48.8 all-gather.9
  117.7 48.8 all-gather.5
where the time goes:
time: 187 us
  waiting for transfers between devices  154 us (82%)
  between operations  13.3 us (7%)
  matrix products  10.4 us (6%)
  starting transfers between devices  4.75 us (3%)
  local copies, waits for them, and re-layouts  2.53 us (1%)
  other arithmetic  1.89 us (1%)
    all_gather x1, waiting for transfers between devices, body(): refl_second = lax.all_gather(refl_local[1], 'blk', axis=0, tiled=True)  53.5 us
    all_gather x1, waiting for transfers between devices, body(): piece_rows = lax.all_gather(trans_local, 'blk', axis=0, tiled=True)  48.1 us
    all_gather x1, waiting for transfers between devices, body(): slab_matrix = lax.all_gather(joined, 'blk', axis=0, tiled=True)  42.3 us
    dot_general x4, matrix products, complex_rows(): product = jnp.dot(stacked, right_matrix, preferred_element_type=jnp.float32)  10.4 us
    ppermute x2, waiting for transfers between devices, shifted(): return lax.ppermute(block, axis, route)  9.38 us
    ppermute x2, starting transfers between devices, shifted(): return lax.ppermute(block, axis, route)  4.67 us
  transfers between devices with their start and end apart: 5, of which 5 were waited for; matrix products, arithmetic and copies ran while one was open for 2% of the time, Pallas kernels for 0%

commit v1 on v0

--- a/solution.py
+++ b/solution.py
@@ -27,13 +27,42 @@
 
 
 def body(transmit, reflect, source_amp, source_cell, source_slab):
+
+    def _search_column(x_part):
+        fresh = lax.axis_size("blk")
+        row_list = []
+        x_new, outer, now = (fresh, lax.axis_index("blk"), x_part.shape[0])
+        for idx, b in enumerate(x_part.shape):
+            row_list.append(b * x_new if idx == 0 else b)
+        current_arr = lax.dynamic_update_slice_in_dim(
+            jnp.zeros(row_list, x_part.dtype), x_part, outer * now, axis=0
+        )
+        high = known = x_part
+        for ii in tuple(range(1, x_new // 2 + 1)):
+            rows = []
+            for idx in tuple(range(x_new)):
+                rows.append((idx, (idx + 1) % x_new))
+            high = lax.ppermute(high, axis_name="blk", perm=rows)
+            current_arr = lax.dynamic_update_slice_in_dim(
+                current_arr, high, (outer - ii) % x_new * now, axis=0
+            )
+            if 2 * ii < x_new:
+                queue = []
+                for idx in [*range(x_new)]:
+                    queue.append((idx, (idx - 1) % x_new))
+                known = lax.ppermute(known, axis_name="blk", perm=queue)
+                current_arr = lax.dynamic_update_slice_in_dim(
+                    current_arr, known, (outer + ii) % x_new * now, axis=0
+                )
+        return current_arr
+
     trans_local = transmit[0]
     refl_local = reflect[0]
     half_width = source_amp.shape[1] // 2
     refl_second = lax.all_gather(refl_local[1], "blk", axis=0, tiled=True)
     coupling = complex_rows(refl_local[0], refl_second).astype(jnp.bfloat16)
     start_rows = trans_local.astype(jnp.float32)
-    piece_rows = lax.all_gather(trans_local, "blk", axis=0, tiled=True)
+    piece_rows = _search_column(trans_local)
     piece_count = piece_rows.shape[0]
     real_cols = lax.slice_in_dim(coupling, 0, piece_count, axis=1)
     imag_cols = lax.dynamic_slice_in_dim(coupling, half_width, piece_count, 1)

time: 187 us -> 164 us (0.88)
  waiting for transfers between devices: 154 us -> 83 us
  starting transfers between devices: 4.75 us -> 38 us
  local copies, waits for them, and re-layouts: 2.53 us -> 16.8 us
    all_gather x1, waiting for transfers between devices: 53.5 us -> 0.01 us  [body(): refl_second = lax.all_gather(refl_local[1], 'blk', axis=0, tiled=True)]
    all_gather x1 -> x0, waiting for transfers between devices: 48.1 us -> none  [body(): piece_rows = lax.all_gather(trans_local, 'blk', axis=0, tiled=True)]
    ppermute x0 -> x15, starting transfers between devices: none -> 34.5 us  [the longest x7 32.4 us: _search_column(): known = lax.ppermute(known, axis_name='blk', perm=queue)]
    ppermute x0 -> x15, waiting for transfers between devices: none -> 32.6 us  [the longest x8 19.5 us: _search_column(): high = lax.ppermute(high, axis_name='blk', perm=rows)]
    dynamic_update_slice x0 -> x16, local copies, waits for them, and re-layouts: none -> 11.7 us  [the longest x8 5.84 us: _search_column(): lax.dynamic_update_slice_in_dim(current_arr, high, (outer - ii) % x_new *...]
    broadcast_in_dim x0 -> x1, local copies, waits for them, and re-layouts: none -> 2.55 us  [_search_column(): jnp.zeros(row_list, x_part.dtype)]
  transfers between devices with their start and end apart: 5 -> 19, of which waited for: 5 -> 14; matrix products, arithmetic and copies ran while one was open for 2% -> 9% of each run, Pallas kernels for 0% -> 0%
where the time goes in v1:
time: 164 us
  waiting for transfers between devices  83 us (51%)
  starting transfers between devices  38 us (23%)
  local copies, waits for them, and re-layouts  16.8 us (10%)
  between operations  13.6 us (8%)
  matrix products  10.4 us (6%)
  other arithmetic  1.89 us (1%)
    all_gather x1, waiting for transfers between devices, body(): slab_matrix = lax.all_gather(joined, 'blk', axis=0, tiled=True)  41.6 us
    ppermute x7, starting transfers between devices, _search_column(): known = lax.ppermute(known, axis_name='blk', perm=queue)  32.4 us
    ppermute x8, waiting for transfers between devices, _search_column(): high = lax.ppermute(high, axis_name='blk', perm=rows)  19.5 us
    ppermute x7, waiting for transfers between devices, _search_column(): known = lax.ppermute(known, axis_name='blk', perm=queue)  13.1 us
    dot_general x4, matrix products, complex_rows(): product = jnp.dot(stacked, right_matrix, preferred_element_type=jnp.float32)  10.4 us
    ppermute x2, waiting for transfers between devices, shifted(): return lax.ppermute(block, axis, route)  8.74 us
    dynamic_update_slice x8, local copies, waits for them, and re-layouts, _search_column(): lax.dynamic_update_slice_in_dim(current_arr, high, (outer - ii) % x_new *...  5.84 us
    dynamic_update_slice x7, local copies, waits for them, and re-layouts, _search_column(): lax.dynamic_update_slice_in_dim(current_arr, known, (outer + ii) % x_new...  5.07 us
  transfers between devices with their start and end apart: 19, of which 14 were waited for; matrix products, arithmetic and copies ran while one was open for 9% of the time, Pallas kernels for 0%

profile of v1, /device:TPU:0, one launch (start us, length us, event | category | flops | bytes accessed | tf_op | source)
XLA Modules:
  0.0 163.7 jit_solution(5955358650885091420)
XLA Ops:
  6.5 1.8 %slice_bitcast_fusion.2 = (bf16[64,2048]{1,0:T(8,128)(2,1)S(1)}, bf16[1,1,64,2048]{3,2,1,0:T(8,128)(2,1)}) fusion(bf16[1,2,64,2048]{3,2,1,0:T(8,128)(2,1)} %param.6), kind=kLoop, calls=%fused_computation.26 | loop fusion | bytes 1048576 | tf_op jit(solution)/shard_map/squeeze | solution.py:63
  9.0 5.0 %collective-permute-start.2 = (bf16[64,2048]{1,0:T(8,128)(2,1)}, bf16[64,2048]{1,0:T(8,128)(2,1)S(1)}, u32[]{:S(2)}, u32[]{:S(2)}) collective-permute-start(bf16[64,2048]{1,0:T(8,128)(2,1)} %bitcast.17), channel_id=1, source_target_pairs={{0,15},{1,0},{2,1},{3,2},{4,3},{5,4},{6,5},{7,6},{8,7},{9,8},{10,9... | collective-permute-start | bytes 786440 | tf_op jit(solution)/shard_map/ppermute | solution.py:53
  14.0 2.6 %broadcast_in_dim.13 = bf16[1024,2048]{1,0:T(8,128)(2,1)} broadcast(bf16[]{:T(256)} %constant.111.clone.1), dimensions={} | broadcast | bytes 4194306 | tf_op jit(solution)/shard_map/broadcast_in_dim | solution.py:38
  18.3 4.4 %collective-permute-start.4 = (bf16[64,2048]{1,0:T(8,128)(2,1)S(1)}, bf16[64,2048]{1,0:T(8,128)(2,1)S(1)}, u32[]{:S(2)}, u32[]{:S(2)}) collective-permute-start(bf16[64,2048]{1,0:T(8,128)(2,1)S(1)} %collective-permute-done.2), channel_id=1, source_target_pairs={{0,15},{1,0},{2,1},{3,2},{4,3},{5,4},{6,5},{7,6},{8,7},{9,8},{10,9... | collective-permute-start | bytes 786440 | tf_op jit(solution)/shard_map/ppermute | solution.py:53
  24.2 4.5 %collective-permute-done.3 = bf16[64,2048]{1,0:T(8,128)(2,1)S(1)} collective-permute-done((bf16[64,2048]{1,0:T(8,128)(2,1)S(1)}, bf16[64,2048]{1,0:T(8,128)(2,1)S(1)}, u32[]{:S(2)}, u32[]{:S(2)}) %collective-permute-start.3) | collective-permute-done | bytes 262176 | tf_op jit(solution)/shard_map/ppermute | solution.py:45
  28.8 4.4 %collective-permute-start.6 = (bf16[64,2048]{1,0:T(8,128)(2,1)S(1)}, bf16[64,2048]{1,0:T(8,128)(2,1)S(1)}, u32[]{:S(2)}, u32[]{:S(2)}) collective-permute-start(bf16[64,2048]{1,0:T(8,128)(2,1)S(1)} %collective-permute-done.4), channel_id=1, source_target_pairs={{0,15},{1,0},{2,1},{3,2},{4,3},{5,4},{6,5},{7,6},{8,7},{9,8},{10,9... | collective-permute-start | bytes 786440 | tf_op jit(solution)/shard_map/ppermute | solution.py:53
  34.6 3.7 %collective-permute-done.5 = bf16[64,2048]{1,0:T(8,128)(2,1)S(1)} collective-permute-done((bf16[64,2048]{1,0:T(8,128)(2,1)S(1)}, bf16[64,2048]{1,0:T(8,128)(2,1)S(1)}, u32[]{:S(2)}, u32[]{:S(2)}) %collective-permute-start.5) | collective-permute-done | bytes 262176 | tf_op jit(solution)/shard_map/ppermute | solution.py:45
  38.4 4.4 %collective-permute-start.8 = (bf16[64,2048]{1,0:T(8,128)(2,1)S(1)}, bf16[64,2048]{1,0:T(8,128)(2,1)S(1)}, u32[]{:S(2)}, u32[]{:S(2)}) collective-permute-start(bf16[64,2048]{1,0:T(8,128)(2,1)S(1)} %collective-permute-done.6), channel_id=1, source_target_pairs={{0,15},{1,0},{2,1},{3,2},{4,3},{5,4},{6,5},{7,6},{8,7},{9,8},{10,9... | collective-permute-start | bytes 786440 | tf_op jit(solution)/shard_map/ppermute | solution.py:53
  44.3 2.7 %collective-permute-done.7 = bf16[64,2048]{1,0:T(8,128)(2,1)S(1)} collective-permute-done((bf16[64,2048]{1,0:T(8,128)(2,1)S(1)}, bf16[64,2048]{1,0:T(8,128)(2,1)S(1)}, u32[]{:S(2)}, u32[]{:S(2)}) %collective-permute-start.7) | collective-permute-done | bytes 262176 | tf_op jit(solution)/shard_map/ppermute | solution.py:45
  47.0 5.2 %collective-permute-done.8 = bf16[64,2048]{1,0:T(8,128)(2,1)S(1)} collective-permute-done((bf16[64,2048]{1,0:T(8,128)(2,1)S(1)}, bf16[64,2048]{1,0:T(8,128)(2,1)S(1)}, u32[]{:S(2)}, u32[]{:S(2)}) %collective-permute-start.8) | collective-permute-done | bytes 262176 | tf_op jit(solution)/shard_map/ppermute | solution.py:53
  52.2 4.6 %collective-permute-start.10 = (bf16[64,2048]{1,0:T(8,128)(2,1)S(1)}, bf16[64,2048]{1,0:T(8,128)(2,1)S(1)}, u32[]{:S(2)}, u32[]{:S(2)}) collective-permute-start(bf16[64,2048]{1,0:T(8,128)(2,1)S(1)} %collective-permute-done.8), channel_id=1, source_target_pairs={{0,15},{1,0},{2,1},{3,2},{4,3},{5,4},{6,5},{7,6},{8,7},{9,8},{10,9... | collective-permute-start | bytes 786440 | tf_op jit(solution)/shard_map/ppermute | solution.py:53
  60.7 4.8 %collective-permute-start.12 = (bf16[64,2048]{1,0:T(8,128)(2,1)S(1)}, bf16[64,2048]{1,0:T(8,128)(2,1)S(1)}, u32[]{:S(2)}, u32[]{:S(2)}) collective-permute-start(bf16[64,2048]{1,0:T(8,128)(2,1)S(1)} %collective-permute-done.10), channel_id=1, source_target_pairs={{0,15},{1,0},{2,1},{3,2},{4,3},{5,4},{6,5},{7,6},{8,7},{9,8},{10,9... | collective-permute-start | bytes 786440 | tf_op jit(solution)/shard_map/ppermute | solution.py:53
  68.3 1.6 collective-permute-start.13
  69.9 4.7 %collective-permute-done.12 = bf16[64,2048]{1,0:T(8,128)(2,1)S(1)} collective-permute-done((bf16[64,2048]{1,0:T(8,128)(2,1)S(1)}, bf16[64,2048]{1,0:T(8,128)(2,1)S(1)}, u32[]{:S(2)}, u32[]{:S(2)}) %collective-permute-start.12) | collective-permute-done | bytes 262176 | tf_op jit(solution)/shard_map/ppermute | solution.py:53
  74.5 4.6 %collective-permute-start.14 = (bf16[64,2048]{1,0:T(8,128)(2,1)S(1)}, bf16[64,2048]{1,0:T(8,128)(2,1)S(1)}, u32[]{:S(2)}, u32[]{:S(2)}) collective-permute-start(bf16[64,2048]{1,0:T(8,128)(2,1)S(1)} %collective-permute-done.12), channel_id=1, source_target_pairs={{0,15},{1,0},{2,1},{3,2},{4,3},{5,4},{6,5},{7,6},{8,7},{9,8},{10,9... | collective-permute-start | bytes 786440 | tf_op jit(solution)/shard_map/ppermute | solution.py:53
  81.3 1.7 %collective-permute-done.14 = bf16[64,2048]{1,0:T(8,128)(2,1)S(1)} collective-permute-done((bf16[64,2048]{1,0:T(8,128)(2,1)S(1)}, bf16[64,2048]{1,0:T(8,128)(2,1)S(1)}, u32[]{:S(2)}, u32[]{:S(2)}) %collective-permute-start.14) | collective-permute-done | bytes 262176 | tf_op jit(solution)/shard_map/ppermute | solution.py:53
  83.7 5.3 %collective-permute-done.15 = bf16[64,2048]{1,0:T(8,128)(2,1)S(1)} collective-permute-done((bf16[64,2048]{1,0:T(8,128)(2,1)S(1)}, bf16[64,2048]{1,0:T(8,128)(2,1)S(1)}, u32[]{:S(2)}, u32[]{:S(2)}) %collective-permute-start.15) | collective-permute-done | bytes 262176 | tf_op jit(solution)/shard_map/ppermute | solution.py:45
  89.8 2.9 %fusion.4 = f32[128,2048]{1,0:T(8,128)S(1)} fusion(bf16[1,1,1024,2048]{3,2,1,0:T(8,128)(2,1)} %all-gather.6.cloned.1.call-done, bf16[64,1024]{1,0:T(8,128)(2,1)S(1)} %get-tuple-element.18, bf16[64,1024]{1,0:T(8,128)(2,1)S(1)} %get-tuple-element.17), kind=kOutput, calls=%fused_computation.4 | convolution fusion | flops 537395200 | bytes 5505024 | tf_op jit(solution)/shard_map/dot_general | solution.py:23
  92.8 3.0 %fusion.12 = f32[128,2048]{1,0:T(8,128)S(1)} fusion(bf16[1024,2048]{1,0:T(8,128)(2,1)} %constant_dynamic-update-slice_fusion, bf16[64,1024]{1,0:T(8,128)(2,1)S(1)} %get-tuple-element.10, bf16[64,1024]{1,0:T(8,128)(2,1)S(1)} %get-tuple-element.9), kind=kOutput, calls=%fused_computation.19 | convolution fusion | flops 537395200 | bytes 5505024 | tf_op jit(solution)/shard_map/dot_general | solution.py:23
  96.8 2.1 %collective-permute-start = (bf16[32,2048]{1,0:T(8,128)(2,1)S(1)}, bf16[32,2048]{1,0:T(8,128)(2,1)S(1)}, u32[]{:S(2)}, u32[]{:S(2)}) collective-permute-start(bf16[32,2048]{1,0:T(8,128)(2,1)S(1)} %add_select_fusion), channel_id=1, source_target_pairs={{0,16},{1,17},{2,18},{3,19},{4,20},{5,21},{6,22},{7,23},{8,24},{9,... | collective-permute-start | bytes 393224 | tf_op jit(solution)/shard_map/ppermute | solution.py:10
  99.0 2.5 %collective-permute-done = bf16[32,2048]{1,0:T(8,128)(2,1)S(1)} collective-permute-done((bf16[32,2048]{1,0:T(8,128)(2,1)S(1)}, bf16[32,2048]{1,0:T(8,128)(2,1)S(1)}, u32[]{:S(2)}, u32[]{:S(2)}) %collective-permute-start) | collective-permute-done | bytes 131104 | tf_op jit(solution)/shard_map/ppermute | solution.py:10
  101.5 41.6 %all-gather.4.cloned.1.call-done = bf16[1024,2048]{1,0:T(8,128)(2,1)} async-done(((bf16[64,2048]{1,0:T(8,128)(2,1)}), bf16[1024,2048]{1,0:T(8,128)(2,1)}) %all-gather.4.cloned.1.call-update) | async-done | bytes 4194320 | tf_op jit(solution)/shard_map/all_gather | solution.py:71
  143.1 3.2 %fusion.21 = f32[64,2048]{1,0:T(8,128)S(1)} fusion(bf16[1024,2048]{1,0:T(8,128)(2,1)} %all-gather.4.cloned.1.call-done, bf16[32,1024]{1,0:T(8,128)(2,1)S(1)} %get-tuple-element.22, bf16[32,1024]{1,0:T(8,128)(2,1)S(1)} %get-tuple-element.21), kind=kOutput, calls=%fused_computation.39 | convolution fusion | flops 268697600 | bytes 4849664 | tf_op jit(solution)/shard_map/dot_general | solution.py:23
  149.9 6.2 %collective-permute-done.16 = bf16[32,2048]{1,0:T(8,128)(2,1)S(1)} collective-permute-done((bf16[32,2048]{1,0:T(8,128)(2,1)S(1)}, bf16[32,2048]{1,0:T(8,128)(2,1)S(1)}, u32[]{:S(2)}, u32[]{:S(2)}) %collective-permute-start.16) | collective-permute-done | bytes 131104 | tf_op jit(solution)/shard_map/ppermute | solution.py:10
  (63 shorter events, 22.4 us)
Async XLA Ops:
  6.5 10.0 %copy-start.1 = (bf16[1,64,2048]{2,1,0:T(8,128)(2,1)S(1)}, bf16[1,64,2048]{2,1,0:T(8,128)(2,1)}, u32[]{:S(2)}) copy-start(bf16[1,64,2048]{2,1,0:T(8,128)(2,1)} %param.5) | copy-start | bytes 786436
  6.5 83.2 %all-gather.6.cloned.1.call-start = ((), (), s32[]{:S(2)}) async-start(), calls=%async_computation.1 | async-start | bytes 4456448 | tf_op jit(solution)/shard_map/all_gather | solution.py:62
  8.4 134.8 %all-gather.4.cloned.1.call-start = ((), (), s32[]{:S(2)}) async-start(), calls=%async_computation | async-start | bytes 4456448 | tf_op jit(solution)/shard_map/all_gather | solution.py:71
  8.4 9.9 %collective-permute-start.1 = (bf16[64,2048]{1,0:T(8,128)(2,1)}, bf16[64,2048]{1,0:T(8,128)(2,1)S(1)}, u32[]{:S(2)}, u32[]{:S(2)}) collective-permute-start(bf16[64,2048]{1,0:T(8,128)(2,1)} %bitcast.16), channel_id=1, source_target_pairs={{0,1},{1,2},{2,3},{3,4},{4,5},{5,6},{6,7},{7,8},{8,9},{9,10},{10,1... | collective-permute-start | bytes 786440 | tf_op jit(solution)/shard_map/ppermute | solution.py:45
  9.0 9.4 %collective-permute-start.2 = (bf16[64,2048]{1,0:T(8,128)(2,1)}, bf16[64,2048]{1,0:T(8,128)(2,1)S(1)}, u32[]{:S(2)}, u32[]{:S(2)}) collective-permute-start(bf16[64,2048]{1,0:T(8,128)(2,1)} %bitcast.17), channel_id=1, source_target_pairs={{0,15},{1,0},{2,1},{3,2},{4,3},{5,4},{6,5},{7,6},{8,7},{9,8},{10,9... | collective-permute-start | bytes 786440 | tf_op jit(solution)/shard_map/ppermute | solution.py:53
  18.3 10.4 %collective-permute-start.3 = (bf16[64,2048]{1,0:T(8,128)(2,1)S(1)}, bf16[64,2048]{1,0:T(8,128)(2,1)S(1)}, u32[]{:S(2)}, u32[]{:S(2)}) collective-permute-start(bf16[64,2048]{1,0:T(8,128)(2,1)S(1)} %collective-permute-done.1), channel_id=1, source_target_pairs={{0,1},{1,2},{2,3},{3,4},{4,5},{5,6},{6,7},{7,8},{8,9},{9,10},{10,1... | collective-permute-start | bytes 786440 | tf_op jit(solution)/shard_map/ppermute | solution.py:45
  18.3 10.4 %collective-permute-start.4 = (bf16[64,2048]{1,0:T(8,128)(2,1)S(1)}, bf16[64,2048]{1,0:T(8,128)(2,1)S(1)}, u32[]{:S(2)}, u32[]{:S(2)}) collective-permute-start(bf16[64,2048]{1,0:T(8,128)(2,1)S(1)} %collective-permute-done.2), channel_id=1, source_target_pairs={{0,15},{1,0},{2,1},{3,2},{4,3},{5,4},{6,5},{7,6},{8,7},{9,8},{10,9... | collective-permute-start | bytes 786440 | tf_op jit(solution)/shard_map/ppermute | solution.py:53
  28.8 9.6 %collective-permute-start.5 = (bf16[64,2048]{1,0:T(8,128)(2,1)S(1)}, bf16[64,2048]{1,0:T(8,128)(2,1)S(1)}, u32[]{:S(2)}, u32[]{:S(2)}) collective-permute-start(bf16[64,2048]{1,0:T(8,128)(2,1)S(1)} %collective-permute-done.3), channel_id=1, source_target_pairs={{0,1},{1,2},{2,3},{3,4},{4,5},{5,6},{6,7},{7,8},{8,9},{9,10},{10,1... | collective-permute-start | bytes 786440 | tf_op jit(solution)/shard_map/ppermute | solution.py:45
  28.8 9.6 %collective-permute-start.6 = (bf16[64,2048]{1,0:T(8,128)(2,1)S(1)}, bf16[64,2048]{1,0:T(8,128)(2,1)S(1)}, u32[]{:S(2)}, u32[]{:S(2)}) collective-permute-start(bf16[64,2048]{1,0:T(8,128)(2,1)S(1)} %collective-permute-done.4), channel_id=1, source_target_pairs={{0,15},{1,0},{2,1},{3,2},{4,3},{5,4},{6,5},{7,6},{8,7},{9,8},{10,9... | collective-permute-start | bytes 786440 | tf_op jit(solution)/shard_map/ppermute | solution.py:53
  38.4 8.6 %collective-permute-start.7 = (bf16[64,2048]{1,0:T(8,128)(2,1)S(1)}, bf16[64,2048]{1,0:T(8,128)(2,1)S(1)}, u32[]{:S(2)}, u32[]{:S(2)}) collective-permute-start(bf16[64,2048]{1,0:T(8,128)(2,1)S(1)} %collective-permute-done.5), channel_id=1, source_target_pairs={{0,1},{1,2},{2,3},{3,4},{4,5},{5,6},{6,7},{7,8},{8,9},{9,10},{10,1... | collective-permute-start | bytes 786440 | tf_op jit(solution)/shard_map/ppermute | solution.py:45
  38.4 13.8 %collective-permute-start.8 = (bf16[64,2048]{1,0:T(8,128)(2,1)S(1)}, bf16[64,2048]{1,0:T(8,128)(2,1)S(1)}, u32[]{:S(2)}, u32[]{:S(2)}) collective-permute-start(bf16[64,2048]{1,0:T(8,128)(2,1)S(1)} %collective-permute-done.6), channel_id=1, source_target_pairs={{0,15},{1,0},{2,1},{3,2},{4,3},{5,4},{6,5},{7,6},{8,7},{9,8},{10,9... | collective-permute-start | bytes 786440 | tf_op jit(solution)/shard_map/ppermute | solution.py:53
  47.0 12.2 %collective-permute-start.9 = (bf16[64,2048]{1,0:T(8,128)(2,1)S(1)}, bf16[64,2048]{1,0:T(8,128)(2,1)S(1)}, u32[]{:S(2)}, u32[]{:S(2)}) collective-permute-start(bf16[64,2048]{1,0:T(8,128)(2,1)S(1)} %collective-permute-done.7), channel_id=1, source_target_pairs={{0,1},{1,2},{2,3},{3,4},{4,5},{5,6},{6,7},{7,8},{8,9},{9,10},{10,1... | collective-permute-start | bytes 786440 | tf_op jit(solution)/shard_map/ppermute | solution.py:45
  52.2 8.5 %collective-permute-start.10 = (bf16[64,2048]{1,0:T(8,128)(2,1)S(1)}, bf16[64,2048]{1,0:T(8,128)(2,1)S(1)}, u32[]{:S(2)}, u32[]{:S(2)}) collective-permute-start(bf16[64,2048]{1,0:T(8,128)(2,1)S(1)} %collective-permute-done.8), channel_id=1, source_target_pairs={{0,15},{1,0},{2,1},{3,2},{4,3},{5,4},{6,5},{7,6},{8,7},{9,8},{10,9... | collective-permute-start | bytes 786440 | tf_op jit(solution)/shard_map/ppermute | solution.py:53
  59.2 9.1 %collective-permute-start.11 = (bf16[64,2048]{1,0:T(8,128)(2,1)S(1)}, bf16[64,2048]{1,0:T(8,128)(2,1)S(1)}, u32[]{:S(2)}, u32[]{:S(2)}) collective-permute-start(bf16[64,2048]{1,0:T(8,128)(2,1)S(1)} %collective-permute-done.9), channel_id=1, source_target_pairs={{0,1},{1,2},{2,3},{3,4},{4,5},{5,6},{6,7},{7,8},{8,9},{9,10},{10,1... | collective-permute-start | bytes 786440 | tf_op jit(solution)/shard_map/ppermute | solution.py:45
  60.7 13.8 %collective-permute-start.12 = (bf16[64,2048]{1,0:T(8,128)(2,1)S(1)}, bf16[64,2048]{1,0:T(8,128)(2,1)S(1)}, u32[]{:S(2)}, u32[]{:S(2)}) collective-permute-start(bf16[64,2048]{1,0:T(8,128)(2,1)S(1)} %collective-permute-done.10), channel_id=1, source_target_pairs={{0,15},{1,0},{2,1},{3,2},{4,3},{5,4},{6,5},{7,6},{8,7},{9,8},{10,9... | collective-permute-start | bytes 786440 | tf_op jit(solution)/shard_map/ppermute | solution.py:53
  68.3 12.3 %collective-permute-start.13 = (bf16[64,2048]{1,0:T(8,128)(2,1)S(1)}, bf16[64,2048]{1,0:T(8,128)(2,1)S(1)}, u32[]{:S(2)}, u32[]{:S(2)}) collective-permute-start(bf16[64,2048]{1,0:T(8,128)(2,1)S(1)} %collective-permute-done.11), channel_id=1, source_target_pairs={{0,1},{1,2},{2,3},{3,4},{4,5},{5,6},{6,7},{7,8},{8,9},{9,10},{10,1... | collective-permute-start | bytes 786440 | tf_op jit(solution)/shard_map/ppermute | solution.py:45
  74.5 8.5 %collective-permute-start.14 = (bf16[64,2048]{1,0:T(8,128)(2,1)S(1)}, bf16[64,2048]{1,0:T(8,128)(2,1)S(1)}, u32[]{:S(2)}, u32[]{:S(2)}) collective-permute-start(bf16[64,2048]{1,0:T(8,128)(2,1)S(1)} %collective-permute-done.12), channel_id=1, source_target_pairs={{0,15},{1,0},{2,1},{3,2},{4,3},{5,4},{6,5},{7,6},{8,7},{9,8},{10,9... | collective-permute-start | bytes 786440 | tf_op jit(solution)/shard_map/ppermute | solution.py:53
  80.6 8.5 %collective-permute-start.15 = (bf16[64,2048]{1,0:T(8,128)(2,1)S(1)}, bf16[64,2048]{1,0:T(8,128)(2,1)S(1)}, u32[]{:S(2)}, u32[]{:S(2)}) collective-permute-start(bf16[64,2048]{1,0:T(8,128)(2,1)S(1)} %collective-permute-done.13), channel_id=1, source_target_pairs={{0,1},{1,2},{2,3},{3,4},{4,5},{5,6},{6,7},{7,8},{8,9},{9,10},{10,1... | collective-permute-start | bytes 786440 | tf_op jit(solution)/shard_map/ppermute | solution.py:45
  92.8 3.9 %copy-start.4 = (s32[32]{0:T(128)S(1)}, s32[32]{0:T(128)}, u32[]{:S(2)}) copy-start(s32[32]{0:T(128)} %param.9) | copy-start | bytes 388
  92.8 3.9 %copy-start.3 = (s32[32]{0:T(128)S(1)}, s32[32]{0:T(128)}, u32[]{:S(2)}) copy-start(s32[32]{0:T(128)} %param.8) | copy-start | bytes 388
  92.8 4.0 %copy-start.2 = (bf16[32,2048]{1,0:T(8,128)(2,1)S(1)}, bf16[32,2048]{1,0:T(8,128)(2,1)}, u32[]{:S(2)}) copy-start(bf16[32,2048]{1,0:T(8,128)(2,1)} %param.7) | copy-start | bytes 393220
  96.8 4.6 %collective-permute-start = (bf16[32,2048]{1,0:T(8,128)(2,1)S(1)}, bf16[32,2048]{1,0:T(8,128)(2,1)S(1)}, u32[]{:S(2)}, u32[]{:S(2)}) collective-permute-start(bf16[32,2048]{1,0:T(8,128)(2,1)S(1)} %add_select_fusion), channel_id=1, source_target_pairs={{0,16},{1,17},{2,18},{3,19},{4,20},{5,21},{6,22},{7,23},{8,24},{9,... | collective-permute-start | bytes 393224 | tf_op jit(solution)/shard_map/ppermute | solution.py:10
  143.1 3.4 %copy-start = (bf16[1024,2048]{1,0:T(8,128)(2,1)S(1)}, bf16[1024,2048]{1,0:T(8,128)(2,1)}, u32[]{:S(2)}) copy-start(bf16[1024,2048]{1,0:T(8,128)(2,1)} %all-gather.4.cloned.1.call-done) | copy-start | bytes 12582916
  148.6 7.5 %collective-permute-start.16 = (bf16[32,2048]{1,0:T(8,128)(2,1)S(1)}, bf16[32,2048]{1,0:T(8,128)(2,1)S(1)}, u32[]{:S(2)}, u32[]{:S(2)}) collective-permute-start(bf16[32,2048]{1,0:T(8,128)(2,1)S(1)} %pad_maximum_fusion), channel_id=1, source_target_pairs={{16,0},{17,1},{18,2},{19,3},{20,4},{21,5},{22,6},{23,7},{24,8},{25... | collective-permute-start | bytes 393224 | tf_op jit(solution)/shard_map/ppermute | solution.py:10
Sparse Core Ops, SparseCore 0:
  9.5 67.6 all-gather.5
  96.7 46.3 all-gather.3
